TPU v7x, 512 devices: a whole 4x4x16 slice. The times are simulated.
512 devices in a mesh: ctx: 64 (over z, y), ch: 8 (over x, core).
Axes of the slice: x: 4, y: 4, z: 16, core: 2. Of those that a mesh axis runs over, the one named last changes fastest.
Arguments:
- query_proj: bfloat16 [16384, 1024], P('ctx', 'ch'), may hold values from -16 to 16
- key_proj: bfloat16 [16384, 1024], P('ctx', 'ch'), may hold values from -8 to 8
- value_proj: bfloat16 [16384, 1024], P('ctx', 'ch'), may hold values from 0.25 to 1.75
- decays: float32 [1024, 16], replicated, may hold values from 1.2207031e-05 to 0.1, as said below
- residues: float32 [1024, 16], replicated, may hold values from -1.5 to 1.5
- skip_gain: float32 [1024], P('ch'), may hold values from -6 to 6
Outputs:
- mixed: bfloat16 [16384, 1024], P('ctx', 'ch')
Inputs may be any that keep to these rules, and one draw needn't show every extreme that they name: `decays`: every rate is positive and no larger than 0.1; each channel has at least one mode slower than 2 / 16384 and one faster.
All inputs are finite; a program needn't handle non-finite values.
Results may differ from a plain program's by a relative error of at most 0.0042.
Values may be sent and summed in bfloat16 or wider, within the bound.
A program may use at most 64 MiB of HBM per device.

v0:
```python
import jax
import jax.numpy as jnp
from jax import lax
from jax.experimental import pallas as pl
from jax.experimental.pallas import tpu as pltpu
from jax.sharding import PartitionSpec as P

MESH = pl.DeviceIdType.MESH
F32 = jnp.float32
ROWS = 8
Y_COUNT = 4


def far_first(count):
    return sorted(range(1, count), key=lambda step: (-min(step, count - step), step))


def kernel(
    query_hbm, key_hbm, value_hbm, decay_hbm, weight_hbm, gain_hbm, out_hbm,
    query_buf, key_buf, value_buf, decay_buf, weight_buf, gain_buf, out_buf,
    signal, shifted, table, taps, base, near, power, prefix,
    own_state, row_states, row_total, column_states,
    load_sems, store_sem, y_send, y_recv, z_send, z_recv,
):
    row_count, lane_count = query_buf.shape
    mode_count = decay_buf.shape[0]
    block_count = row_count // ROWS
    ctx_count = lax.axis_size("ctx")
    z_count = ctx_count // Y_COUNT
    ctx = lax.axis_index("ctx")
    z_at = ctx // Y_COUNT
    y_at = ctx % Y_COUNT
    lanes = pl.ds(pl.multiple_of(lax.axis_index("ch") * lane_count, lane_count), lane_count)

    loads = [
        pltpu.make_async_copy(source, target, load_sems.at[slot])
        for slot, (source, target) in enumerate(
            [
                (decay_hbm.at[:, lanes], decay_buf),
                (key_hbm, key_buf),
                (value_hbm, value_buf),
                (weight_hbm.at[:, lanes], weight_buf),
                (gain_hbm, gain_buf),
                (query_hbm, query_buf),
            ]
        )
    ]
    for load in loads:
        load.start()

    barrier = pltpu.get_barrier_semaphore()
    for step in range(1, Y_COUNT):
        peer = z_at * Y_COUNT + (y_at + step) % Y_COUNT
        pl.semaphore_signal(barrier, inc=1, device_id={"ctx": peer}, device_id_type=MESH)
    for step in far_first(z_count):

        @pl.when(z_at >= step)
        def _(step=step):
            peer = ctx - step * Y_COUNT
            pl.semaphore_signal(barrier, inc=1, device_id={"ctx": peer}, device_id_type=MESH)

    loads[0].wait()
    decay = decay_buf[...]
    loads[1].wait()
    loads[2].wait()
    product = key_buf[...].astype(F32) * value_buf[...].astype(F32)
    signal[0:64, :] = jnp.zeros((64, lane_count), F32)
    signal[64:, :] = product.astype(jnp.bfloat16).astype(F32)
    sub = lax.broadcasted_iota(jnp.int32, (ROWS, lane_count), 0).astype(F32)
    rate = [jnp.broadcast_to(decay_buf[r : r + 1, :], (ROWS, lane_count)) for r in range(mode_count)]
    leap = [jnp.exp(-float(ROWS) * rate[r]) for r in range(mode_count)]

    def gather(block, sums):
        rows = signal[pl.ds(pl.multiple_of(64 + ROWS * block, ROWS), ROWS), :]
        return tuple(leap[r] * sums[r] + rows for r in range(mode_count))

    sums = lax.fori_loop(
        0, block_count, gather, (jnp.zeros((ROWS, lane_count), F32),) * mode_count, unroll=4
    )
    for r in range(mode_count):
        fade = jnp.exp(-rate[r] * (float(ROWS - 1) - sub))
        own_state[r : r + 1, :] = jnp.sum(sums[r] * fade, axis=0, keepdims=True)

    pl.semaphore_wait(barrier, Y_COUNT - 1 + (z_count - 1 - z_at))

    y_copies = []
    for step in range(1, Y_COUNT):
        peer_y = (y_at + step) % Y_COUNT
        copy = pltpu.make_async_remote_copy(
            src_ref=own_state,
            dst_ref=row_states.at[step],
            send_sem=y_send.at[step],
            recv_sem=y_recv.at[step],
            device_id={"ctx": z_at * Y_COUNT + peer_y},
            device_id_type=MESH,
        )
        copy.start()
        y_copies.append(copy)
    span = float(row_count)
    for step in range(1, z_count):
        power[step] = jnp.exp(decay * (-span * Y_COUNT * (step - 1)))
    y_f = y_at.astype(F32)
    for copy in y_copies:
        copy.wait_recv()
    total = own_state[...] * jnp.exp(decay * (-span * (Y_COUNT - 1 - y_f)))
    before = jnp.zeros_like(decay)
    for step in range(1, Y_COUNT):
        source = (y_at - step + Y_COUNT) % Y_COUNT
        state = row_states[step]
        total = total + state * jnp.exp(decay * (-span * (Y_COUNT - 1 - source.astype(F32))))
        ahead = jnp.maximum(y_at - 1 - source, 0).astype(F32)
        seen = jnp.where(source < y_at, 1.0, 0.0)
        before = before + state * (seen * jnp.exp(decay * (-span * ahead)))
    row_total[...] = total
    prefix[...] = before

    def z_copy(step):
        return pltpu.make_async_remote_copy(
            src_ref=row_total,
            dst_ref=column_states.at[step],
            send_sem=z_send.at[step],
            recv_sem=z_recv.at[step],
            device_id={"ctx": lax.rem(ctx + step * Y_COUNT, ctx_count)},
            device_id_type=MESH,
        )

    for step in far_first(z_count):

        @pl.when(z_at + step < z_count)
        def _(step=step):
            z_copy(step).start()

    loads[3].wait()
    loads[4].wait()
    weight = weight_buf[...] * jnp.sqrt(2.0 * decay)
    weight_buf[...] = weight
    start = tuple(weight_buf[r : r + 1, :] * jnp.exp(-rate[r] * sub) for r in range(mode_count))

    def tabulate(block, modes):
        total = modes[0]
        for r in range(1, mode_count):
            total = total + modes[r]
        taps[pl.ds(pl.multiple_of(ROWS * block, ROWS), ROWS), :] = total
        for r in range(mode_count):
            table[block, r] = modes[r]
        return tuple(modes[r] * leap[r] for r in range(mode_count))

    lax.fori_loop(0, block_count, tabulate, start)

    for shift in range(ROWS):
        shifted[shift, 0:56, :] = jnp.zeros((56, lane_count), F32)
        shifted[shift, 56:, :] = signal[64 - shift : 64 + row_count - shift, :]
    gain = gain_buf[...]
    for group in range(row_count // 64):

        def slide(lag, sums, group=group):
            for shift in range(ROWS):
                tap = taps[pl.ds(lag * ROWS + shift, 1), :]
                rows = shifted[shift, pl.ds(pl.multiple_of(64 * group + 56 - ROWS * lag, ROWS), 64), :]
                sums = sums + tap * rows
            return sums

        rows = slice(64 * group, 64 * group + 64)
        first = gain * signal[64 + 64 * group : 128 + 64 * group, :]
        base[rows, :] = lax.fori_loop(0, 8 * group + 8, slide, first)
    loads[5].wait()

    near[...] = jnp.zeros_like(decay)
    for step in range(1, z_count):

        @pl.when(z_at >= step)
        def _(step=step):
            z_copy(step).wait_recv()
            near[...] += power[step] * column_states[step]

    entering = prefix[...] + near[...] * jnp.exp(decay * (-span * y_f))
    near[...] = entering * jnp.exp(-decay)
    modes = [jnp.broadcast_to(near[r : r + 1, :], (ROWS, lane_count)) for r in range(mode_count)]

    def finish(pair, carry):
        tiles = []
        for half in range(2):
            block = 2 * pair + half
            total = base[pl.ds(pl.multiple_of(ROWS * block, ROWS), ROWS), :]
            for r in range(mode_count):
                total = total + table[block, r] * modes[r]
            tiles.append(total)
        rows = pl.ds(pl.multiple_of(2 * ROWS * pair, 2 * ROWS), 2 * ROWS)
        mixed = query_buf[rows, :].astype(F32) * jnp.concatenate(tiles, axis=0)
        out_buf[rows, :] = mixed.astype(jnp.bfloat16)
        return carry

    lax.fori_loop(0, block_count // 2, finish, 0)
    store = pltpu.make_async_copy(out_buf, out_hbm, store_sem)
    store.start()
    for copy in y_copies:
        copy.wait_send()
    for step in range(1, z_count):

        @pl.when(z_at + step < z_count)
        def _(step=step):
            z_copy(step).wait_send()

    store.wait()


def local(query_proj, key_proj, value_proj, decays, residues, skip_gain):
    row_count, lane_count = query_proj.shape
    mode_count = decays.shape[1]
    ctx_count = lax.axis_size("ctx")
    z_count = ctx_count // Y_COUNT
    state = (mode_count, lane_count)
    wide = (row_count, lane_count)
    block_count = row_count // ROWS
    any_space = pl.BlockSpec(memory_space=pl.ANY)
    return pl.pallas_call(
        kernel,
        out_shape=jax.ShapeDtypeStruct(wide, jnp.bfloat16),
        in_specs=[any_space] * 6,
        out_specs=any_space,
        scratch_shapes=[
            pltpu.VMEM(wide, jnp.bfloat16),
            pltpu.VMEM(wide, jnp.bfloat16),
            pltpu.VMEM(wide, jnp.bfloat16),
            pltpu.VMEM(state, F32),
            pltpu.VMEM(state, F32),
            pltpu.VMEM((1, lane_count), F32),
            pltpu.VMEM(wide, jnp.bfloat16),
            pltpu.VMEM((64 + row_count, lane_count), F32),
            pltpu.VMEM((ROWS, 56 + row_count, lane_count), F32),
            pltpu.VMEM((block_count, mode_count, ROWS, lane_count), F32),
            pltpu.VMEM(wide, F32),
            pltpu.VMEM(wide, F32),
            pltpu.VMEM(state, F32),
            pltpu.VMEM((z_count,) + state, F32),
            pltpu.VMEM(state, F32),
            pltpu.VMEM(state, F32),
            pltpu.VMEM((Y_COUNT,) + state, F32),
            pltpu.VMEM(state, F32),
            pltpu.VMEM((z_count,) + state, F32),
            pltpu.SemaphoreType.DMA((6,)),
            pltpu.SemaphoreType.DMA,
            pltpu.SemaphoreType.DMA((Y_COUNT,)),
            pltpu.SemaphoreType.DMA((Y_COUNT,)),
            pltpu.SemaphoreType.DMA((z_count,)),
            pltpu.SemaphoreType.DMA((z_count,)),
        ],
        compiler_params=pltpu.CompilerParams(collective_id=0, has_side_effects=True),
    )(query_proj, key_proj, value_proj, decays.T, residues.T, skip_gain.reshape(1, lane_count))


def solution(mesh):
    return jax.shard_map(
        local,
        mesh=mesh,
        in_specs=(P("ctx", "ch"), P("ctx", "ch"), P("ctx", "ch"), P(), P(), P("ch")),
        out_specs=P("ctx", "ch"),
        check_vma=False,
    )
```

profile of v0, /device:TPU:4, one launch (start us, length us, event | category | flops | bytes accessed | tf_op | source)
XLA Modules:
  0.0 26.1 jit_solution(9511433737145695629)
XLA Ops:
  0.0 24.6 %shard_map.64 = bf16[256,128]{1,0:T(8,128)(2,1)} custom-call(bf16[256,128]{1,0:T(8,128)(2,1)} %query_hbm.1, bf16[256,128]{1,0:T(8,128)(2,1)} %key_hbm.1, bf16[256,128]{1,0:T(8,128)(2,1)} %value_hbm.1, f32[16,1024]{1,0:T(8,128)} %bitcast.3, f32[16,1024]{1,0:T(8,128)} %bitcast.4, f32[1,128]{1,0:T(1,128)} %bitcast.5), custom_call_target="tpu_custom_call" | custom-call | tf_op jit(solution)/shard_map/pallas_call | solution.py:216
  24.6 1.5 %copy.8 = bf16[256,128]{1,0:T(8,128)(2,1)} copy(bf16[256,128]{1,0:T(8,128)(2,1)} %shard_map.64) | data formatting | bytes 131072
where the time goes:
time: 26.3 us; the launch traced here: 26.1 us
  Pallas kernels  24.6 us (94%)
  local copies, waits for them, and re-layouts  1.47 us (6%)
    pallas_call x1, Pallas kernels, local(): pl.pallas_call(kernel, out_shape=jax.ShapeDtypeStruct(wide, jnp.bfloat16)...  24.6 us
    unnamed x1, local copies, waits for them, and re-layouts  1.47 us

commit v1 on v0

--- a/solution.py
+++ b/solution.py
@@ -9,6 +9,17 @@
 F32 = jnp.float32
 ROWS = 8
 Y_COUNT = 4
+FIRST_END = 4
+SECOND_END = 7
+HUB = 10
+
+
+def last_target(z_at, z_count):
+    return jnp.where(z_at < FIRST_END - 1, FIRST_END - 1, jnp.where(z_at < SECOND_END - 1, SECOND_END - 1, z_count - 1))
+
+
+def first_source(z_at):
+    return jnp.where(z_at < FIRST_END, 0, jnp.where(z_at < SECOND_END, FIRST_END - 1, SECOND_END - 1))
 
 
 def far_first(count):
@@ -20,7 +31,7 @@
     query_buf, key_buf, value_buf, decay_buf, weight_buf, gain_buf, out_buf,
     signal, shifted, table, taps, base, near, power, prefix,
     own_state, row_states, row_total, column_states,
-    load_sems, store_sem, y_send, y_recv, z_send, z_recv,
+    load_sems, store_sem, y_send, y_recv, z_send, z_recv, ready, go,
 ):
     row_count, lane_count = query_buf.shape
     mode_count = decay_buf.shape[0]
@@ -49,15 +60,27 @@
         load.start()
 
     barrier = pltpu.get_barrier_semaphore()
+    target_end = last_target(z_at, z_count)
+    source_start = first_source(z_at)
+    early_sender = z_at < SECOND_END - 1
+    early_target = z_at < SECOND_END
+    late_member = jnp.logical_and(z_at >= SECOND_END - 1, z_at != HUB)
+    forwards = jnp.logical_or(z_at == FIRST_END - 1, z_at == SECOND_END - 1)
+
+    def tell(semaphore, peer):
+        pl.semaphore_signal(semaphore, inc=1, device_id={"ctx": peer}, device_id_type=MESH)
+
     for step in range(1, Y_COUNT):
-        peer = z_at * Y_COUNT + (y_at + step) % Y_COUNT
-        pl.semaphore_signal(barrier, inc=1, device_id={"ctx": peer}, device_id_type=MESH)
-    for step in far_first(z_count):
-
-        @pl.when(z_at >= step)
+        tell(barrier, z_at * Y_COUNT + (y_at + step) % Y_COUNT)
+    for step in range(1, FIRST_END):
+
+        @pl.when(jnp.logical_and(early_sender, z_at + step <= target_end))
         def _(step=step):
-            peer = ctx - step * Y_COUNT
-            pl.semaphore_signal(barrier, inc=1, device_id={"ctx": peer}, device_id_type=MESH)
+            tell(barrier, ctx + step * Y_COUNT)
+
+    @pl.when(late_member)
+    def _():
+        tell(barrier, HUB * Y_COUNT + y_at)
 
     loads[0].wait()
     decay = decay_buf[...]
@@ -81,7 +104,21 @@
         fade = jnp.exp(-rate[r] * (float(ROWS - 1) - sub))
         own_state[r : r + 1, :] = jnp.sum(sums[r] * fade, axis=0, keepdims=True)
 
-    pl.semaphore_wait(barrier, Y_COUNT - 1 + (z_count - 1 - z_at))
+    greeted = jnp.where(early_target, z_at - source_start, 0)
+    greeted = jnp.where(z_at == HUB, z_count - SECOND_END, greeted)
+    pl.semaphore_wait(barrier, Y_COUNT - 1 + greeted)
+
+    for step in range(1, FIRST_END):
+
+        @pl.when(jnp.logical_and(early_target, z_at - step >= source_start))
+        def _(step=step):
+            tell(ready.at[step], ctx - step * Y_COUNT)
+
+    @pl.when(z_at == HUB)
+    def _():
+        for row in range(SECOND_END - 1, z_count - 1):
+            if row != HUB:
+                tell(go, row * Y_COUNT + y_at)
 
     y_copies = []
     for step in range(1, Y_COUNT):
@@ -99,6 +136,41 @@
     span = float(row_count)
     for step in range(1, z_count):
         power[step] = jnp.exp(decay * (-span * Y_COUNT * (step - 1)))
+    loads[3].wait()
+    loads[4].wait()
+    weight = weight_buf[...] * jnp.sqrt(2.0 * decay)
+    weight_buf[...] = weight
+    start = tuple(weight_buf[r : r + 1, :] * jnp.exp(-rate[r] * sub) for r in range(mode_count))
+
+    def tabulate(block, modes):
+        total = modes[0]
+        for r in range(1, mode_count):
+            total = total + modes[r]
+        taps[pl.ds(pl.multiple_of(ROWS * block, ROWS), ROWS), :] = total
+        for r in range(mode_count):
+            table[block, r] = modes[r]
+        return tuple(modes[r] * leap[r] for r in range(mode_count))
+
+    lax.fori_loop(0, block_count, tabulate, start)
+
+    for shift in range(ROWS):
+        shifted[shift, 0:56, :] = jnp.zeros((56, lane_count), F32)
+        shifted[shift, 56:, :] = signal[64 - shift : 64 + row_count - shift, :]
+    gain = gain_buf[...]
+    for group in range(row_count // 64):
+
+        def slide(lag, sums, group=group):
+            for shift in range(ROWS):
+                tap = taps[pl.ds(lag * ROWS + shift, 1), :]
+                rows = shifted[shift, pl.ds(pl.multiple_of(64 * group + 56 - ROWS * lag, ROWS), 64), :]
+                sums = sums + tap * rows
+            return sums
+
+        rows = slice(64 * group, 64 * group + 64)
+        first = gain * signal[64 + 64 * group : 128 + 64 * group, :]
+        base[rows, :] = lax.fori_loop(0, 8 * group + 8, slide, first)
+    loads[5].wait()
+
     y_f = y_at.astype(F32)
     for copy in y_copies:
         copy.wait_recv()
@@ -124,54 +196,40 @@
             device_id_type=MESH,
         )
 
+    near[...] = jnp.zeros_like(decay)
+
+    def collect():
+        for step in range(1, z_count):
+
+            @pl.when(z_at - step >= source_start)
+            def _(step=step):
+                z_copy(step).wait_recv()
+                near[...] += power[step] * column_states[step]
+
+    @pl.when(forwards)
+    def _():
+        collect()
+        row_total[...] += power[2] * near[...]
+
+    @pl.when(jnp.logical_and(late_member, z_at < z_count - 1))
+    def _():
+        pl.semaphore_wait(go, 1)
+
     for step in far_first(z_count):
 
-        @pl.when(z_at + step < z_count)
+        @pl.when(z_at + step <= target_end)
         def _(step=step):
+            if step < FIRST_END:
+
+                @pl.when(early_sender)
+                def _():
+                    pl.semaphore_wait(ready.at[step], 1)
+
             z_copy(step).start()
 
-    loads[3].wait()
-    loads[4].wait()
-    weight = weight_buf[...] * jnp.sqrt(2.0 * decay)
-    weight_buf[...] = weight
-    start = tuple(weight_buf[r : r + 1, :] * jnp.exp(-rate[r] * sub) for r in range(mode_count))
-
-    def tabulate(block, modes):
-        total = modes[0]
-        for r in range(1, mode_count):
-            total = total + modes[r]
-        taps[pl.ds(pl.multiple_of(ROWS * block, ROWS), ROWS), :] = total
-        for r in range(mode_count):
-            table[block, r] = modes[r]
-        return tuple(modes[r] * leap[r] for r in range(mode_count))
-
-    lax.fori_loop(0, block_count, tabulate, start)
-
-    for shift in range(ROWS):
-        shifted[shift, 0:56, :] = jnp.zeros((56, lane_count), F32)
-        shifted[shift, 56:, :] = signal[64 - shift : 64 + row_count - shift, :]
-    gain = gain_buf[...]
-    for group in range(row_count // 64):
-
-        def slide(lag, sums, group=group):
-            for shift in range(ROWS):
-                tap = taps[pl.ds(lag * ROWS + shift, 1), :]
-                rows = shifted[shift, pl.ds(pl.multiple_of(64 * group + 56 - ROWS * lag, ROWS), 64), :]
-                sums = sums + tap * rows
-            return sums
-
-        rows = slice(64 * group, 64 * group + 64)
-        first = gain * signal[64 + 64 * group : 128 + 64 * group, :]
-        base[rows, :] = lax.fori_loop(0, 8 * group + 8, slide, first)
-    loads[5].wait()
-
-    near[...] = jnp.zeros_like(decay)
-    for step in range(1, z_count):
-
-        @pl.when(z_at >= step)
-        def _(step=step):
-            z_copy(step).wait_recv()
-            near[...] += power[step] * column_states[step]
+    @pl.when(jnp.logical_not(forwards))
+    def _():
+        collect()
 
     entering = prefix[...] + near[...] * jnp.exp(decay * (-span * y_f))
     near[...] = entering * jnp.exp(-decay)
@@ -181,23 +239,24 @@
         tiles = []
         for half in range(2):
             block = 2 * pair + half
-            total = base[pl.ds(pl.multiple_of(ROWS * block, ROWS), ROWS), :]
-            for r in range(mode_count):
-                total = total + table[block, r] * modes[r]
-            tiles.append(total)
+            terms = [table[block, r] * modes[r] for r in range(mode_count)]
+            terms.append(base[pl.ds(pl.multiple_of(ROWS * block, ROWS), ROWS), :])
+            while len(terms) > 1:
+                terms = [sum(terms[at : at + 2][1:], terms[at]) for at in range(0, len(terms), 2)]
+            tiles.append(terms[0])
         rows = pl.ds(pl.multiple_of(2 * ROWS * pair, 2 * ROWS), 2 * ROWS)
         mixed = query_buf[rows, :].astype(F32) * jnp.concatenate(tiles, axis=0)
         out_buf[rows, :] = mixed.astype(jnp.bfloat16)
         return carry
 
-    lax.fori_loop(0, block_count // 2, finish, 0)
+    lax.fori_loop(0, block_count // 2, finish, 0, unroll=2)
     store = pltpu.make_async_copy(out_buf, out_hbm, store_sem)
     store.start()
     for copy in y_copies:
         copy.wait_send()
     for step in range(1, z_count):
 
-        @pl.when(z_at + step < z_count)
+        @pl.when(z_at + step <= target_end)
         def _(step=step):
             z_copy(step).wait_send()
 
@@ -244,6 +303,8 @@
             pltpu.SemaphoreType.DMA((Y_COUNT,)),
             pltpu.SemaphoreType.DMA((z_count,)),
             pltpu.SemaphoreType.DMA((z_count,)),
+            pltpu.SemaphoreType.REGULAR((FIRST_END,)),
+            pltpu.SemaphoreType.REGULAR,
         ],
         compiler_params=pltpu.CompilerParams(collective_id=0, has_side_effects=True),
     )(query_proj, key_proj, value_proj, decays.T, residues.T, skip_gain.reshape(1, lane_count))

time: 26.3 us -> 21.3 us (0.81)
  the two profiles are of different devices: /device:TPU:4 before, /device:TPU:448 now
where the time goes in v1:
time: 21.3 us; the launch traced here: 21.1 us
  Pallas kernels  19.6 us (92%)
  local copies, waits for them, and re-layouts  1.47 us (7%)
    pallas_call x1, Pallas kernels, local(): pl.pallas_call(kernel, out_shape=jax.ShapeDtypeStruct(wide, jnp.bfloat16)...  19.6 us
    unnamed x1, local copies, waits for them, and re-layouts  1.47 us

profile of v1, /device:TPU:448, one launch (start us, length us, event | category | flops | bytes accessed | tf_op | source)
XLA Modules:
  0.0 21.1 jit_solution(4217569525660728964)
XLA Ops:
  0.0 19.6 %shard_map.64 = bf16[256,128]{1,0:T(8,128)(2,1)} custom-call(bf16[256,128]{1,0:T(8,128)(2,1)} %query_hbm.1, bf16[256,128]{1,0:T(8,128)(2,1)} %key_hbm.1, bf16[256,128]{1,0:T(8,128)(2,1)} %value_hbm.1, f32[16,1024]{1,0:T(8,128)} %bitcast.3, f32[16,1024]{1,0:T(8,128)} %bitcast.4, f32[1,128]{1,0:T(1,128)} %bitcast.5), custom_call_target="tpu_custom_call" | custom-call | tf_op jit(solution)/shard_map/pallas_call | solution.py:275
  19.6 1.5 %copy.8 = bf16[256,128]{1,0:T(8,128)(2,1)} copy(bf16[256,128]{1,0:T(8,128)(2,1)} %shard_map.64) | data formatting | bytes 131072

commit v2 on v0

v2 whole, which is shorter than its diff:
```python
import jax
import jax.numpy as jnp
from jax import lax
from jax.experimental import pallas as pl
from jax.experimental.pallas import tpu as pltpu
from jax.sharding import PartitionSpec as P

MESH = pl.DeviceIdType.MESH
F32 = jnp.float32
ROWS = 8
Y_COUNT = 4
FIRST_END = 4
EARLY_END = 7
HUB = 10
NEAR = (1, 2, 3, 4, 5, 6)
FAR = (15, 14, 13, 12, 7, 11)
RELAYED = (8, 11)


def kernel(
    query_hbm, key_hbm, value_hbm, decay_hbm, weight_hbm, gain_hbm, out_hbm,
    query_buf, key_buf, value_buf, decay_buf, weight_buf, gain_buf, out_buf,
    signal, shifted, table, taps, base, near, power, prefix,
    own_state, row_states, row_total, column_states, zero_state,
    load_sems, store_sem, y_send, y_recv, z_send, z_recv, row_ready, ready, go,
    zero_send, zero_recv, zero_ready,
):
    row_count, lane_count = query_buf.shape
    mode_count = decay_buf.shape[0]
    block_count = row_count // ROWS
    ctx_count = lax.axis_size("ctx")
    z_count = ctx_count // Y_COUNT
    ctx = lax.axis_index("ctx")
    z_at = lax.div(ctx, Y_COUNT)
    y_at = ctx - z_at * Y_COUNT
    last = z_count - 1
    early_sender = z_at < EARLY_END - 1
    early_target = z_at < EARLY_END
    apart = lax.axis_index("ch") == 0
    zero = z_at == 0
    target_end = jnp.where(
        z_at < FIRST_END - 1, FIRST_END - 1, jnp.where(early_sender, EARLY_END - 1, last)
    )
    source_start = jnp.where(
        z_at < FIRST_END,
        jnp.where(apart, 1, 0),
        jnp.where(early_target, FIRST_END - 1, EARLY_END - 1),
    )
    send_count = jnp.where(jnp.logical_and(apart, zero), 0, target_end - z_at)
    recv_count = jnp.maximum(z_at - source_start, 0)
    order = jnp.where(jnp.logical_and(apart, zero), lax.rem(y_at + Y_COUNT - 1, Y_COUNT), y_at)
    zero_sender = jnp.logical_and(jnp.logical_and(apart, zero), y_at > 0)
    zero_double = jnp.logical_and(zero_sender, y_at == 1)
    from_zero = jnp.logical_and(apart, z_at > 0)
    direct = jnp.logical_and(from_zero, jnp.logical_or(z_at < RELAYED[0], z_at >= RELAYED[1]))
    relays = jnp.logical_and(apart, z_at == EARLY_END - 1)
    late_member = jnp.logical_and(z_at >= EARLY_END - 1, z_at != HUB)
    forwards = jnp.logical_or(z_at == FIRST_END - 1, z_at == EARLY_END - 1)
    lanes = pl.ds(pl.multiple_of(lax.axis_index("ch") * lane_count, lane_count), lane_count)

    loads = [
        pltpu.make_async_copy(source, target, load_sems.at[slot])
        for slot, (source, target) in enumerate(
            [
                (decay_hbm.at[:, lanes], decay_buf),
                (key_hbm, key_buf),
                (value_hbm, value_buf),
                (weight_hbm.at[:, lanes], weight_buf),
                (gain_hbm, gain_buf),
                (query_hbm, query_buf),
            ]
        )
    ]
    for load in loads:
        load.start()

    barrier = pltpu.get_barrier_semaphore()

    def tell(semaphore, peer):
        pl.semaphore_signal(semaphore, inc=1, device_id={"ctx": peer}, device_id_type=MESH)

    for step in range(1, Y_COUNT):

        @pl.when(order + step < Y_COUNT)
        def _(step=step):
            tell(barrier, z_at * Y_COUNT + lax.rem(y_at + step, Y_COUNT))

    @pl.when(early_sender)
    def _():
        def greet(step, carry):
            tell(barrier, ctx + step * Y_COUNT)
            return carry

        lax.fori_loop(1, send_count + 1, greet, 0)

    @pl.when(zero_sender)
    def _():
        def greet(row, carry):
            tell(barrier, row * Y_COUNT + y_at)
            return carry

        lax.fori_loop(1, RELAYED[0], greet, 0)
        lax.fori_loop(RELAYED[1], z_count, greet, 0)

    @pl.when(zero_double)
    def _():
        def greet(row, carry):
            tell(barrier, row * Y_COUNT)
            return carry

        lax.fori_loop(1, RELAYED[0], greet, 0)
        lax.fori_loop(RELAYED[1], z_count, greet, 0)

    @pl.when(late_member)
    def _():
        tell(barrier, HUB * Y_COUNT + y_at)

    greeted = jnp.where(early_target, recv_count, 0)
    greeted = jnp.where(z_at == HUB, z_count - EARLY_END, greeted)
    greeted = order + greeted + jnp.where(direct, 1, 0)

    @pl.when(greeted > 0)
    def _():
        pl.semaphore_wait(barrier, greeted)

    for step in range(1, Y_COUNT):

        @pl.when(order >= step)
        def _(step=step):
            tell(row_ready.at[step], z_at * Y_COUNT + lax.rem(y_at + Y_COUNT - step, Y_COUNT))

    @pl.when(early_target)
    def _():
        def answer(step, carry):
            tell(ready.at[step], ctx - step * Y_COUNT)
            return carry

        lax.fori_loop(1, recv_count + 1, answer, 0)

    @pl.when(direct)
    def _():
        tell(zero_ready.at[jnp.where(y_at == 0, 1, 0), z_at], jnp.maximum(y_at, 1))

    @pl.when(z_at == HUB)
    def _():
        for row in range(EARLY_END - 1, last):
            if row != HUB:
                tell(go, row * Y_COUNT + y_at)

    loads[0].wait()
    decay = decay_buf[...]
    loads[1].wait()
    loads[2].wait()
    product = key_buf[...].astype(F32) * value_buf[...].astype(F32)
    signal[0:64, :] = jnp.zeros((64, lane_count), F32)
    signal[64:, :] = product.astype(jnp.bfloat16).astype(F32)
    sub = lax.broadcasted_iota(jnp.int32, (ROWS, lane_count), 0).astype(F32)
    rate = [jnp.broadcast_to(decay_buf[r : r + 1, :], (ROWS, lane_count)) for r in range(mode_count)]
    leap = [jnp.exp(-float(ROWS) * rate[r]) for r in range(mode_count)]

    def gather(block, sums):
        rows = signal[pl.ds(pl.multiple_of(64 + ROWS * block, ROWS), ROWS), :]
        return tuple(leap[r] * sums[r] + rows for r in range(mode_count))

    sums = lax.fori_loop(
        0, block_count, gather, (jnp.zeros((ROWS, lane_count), F32),) * mode_count, unroll=4
    )
    for r in range(mode_count):
        fade = jnp.exp(-rate[r] * (float(ROWS - 1) - sub))
        own_state[r : r + 1, :] = jnp.sum(sums[r] * fade, axis=0, keepdims=True)

    def y_copy(step):
        peer_y = lax.rem(y_at + step, Y_COUNT)
        return pltpu.make_async_remote_copy(
            src_ref=own_state,
            dst_ref=row_states.at[step],
            send_sem=y_send.at[step],
            recv_sem=y_recv.at[step],
            device_id={"ctx": z_at * Y_COUNT + peer_y},
            device_id_type=MESH,
        )

    for step in range(1, Y_COUNT):

        @pl.when(order + step >= Y_COUNT)
        def _(step=step):
            y_copy(step).start()

    for step in range(1, Y_COUNT):

        @pl.when(order + step < Y_COUNT)
        def _(step=step):
            pl.semaphore_wait(row_ready.at[step], 1)
            y_copy(step).start()

    span = float(row_count)
    for step in range(1, z_count):
        power[step] = jnp.exp(decay * (-span * Y_COUNT * (step - 1)))
    def convolve():
        loads[3].wait()
        loads[4].wait()
        weight = weight_buf[...] * jnp.sqrt(2.0 * decay)
        weight_buf[...] = weight
        start = tuple(weight_buf[r : r + 1, :] * jnp.exp(-rate[r] * sub) for r in range(mode_count))

        def tabulate(block, modes):
            total = modes[0]
            for r in range(1, mode_count):
                total = total + modes[r]
            taps[pl.ds(pl.multiple_of(ROWS * block, ROWS), ROWS), :] = total
            for r in range(mode_count):
                table[block, r] = modes[r]
            return tuple(modes[r] * leap[r] for r in range(mode_count))

        lax.fori_loop(0, block_count, tabulate, start)

        for shift in range(ROWS):
            shifted[shift, 0:56, :] = jnp.zeros((56, lane_count), F32)
            shifted[shift, 56:, :] = signal[64 - shift : 64 + row_count - shift, :]
        gain = gain_buf[...]
        for group in range(row_count // 64):

            def slide(lag, sums, group=group):
                for shift in range(ROWS):
                    tap = taps[pl.ds(lag * ROWS + shift, 1), :]
                    rows = shifted[shift, pl.ds(pl.multiple_of(64 * group + 56 - ROWS * lag, ROWS), 64), :]
                    sums = sums + tap * rows
                return sums

            rows = slice(64 * group, 64 * group + 64)
            first = gain * signal[64 + 64 * group : 128 + 64 * group, :]
            base[rows, :] = lax.fori_loop(0, 8 * group + 8, slide, first)
        loads[5].wait()

    @pl.when(zero)
    def _():
        convolve()

    y_f = y_at.astype(F32)
    whole, ahead = [], []
    for step in range(Y_COUNT):
        source = lax.rem(y_at - step + Y_COUNT, Y_COUNT)
        whole.append(jnp.exp(decay * (-span * (Y_COUNT - 1 - source).astype(F32))))
        seen = jnp.where(source < y_at, 1.0, 0.0)
        gap = jnp.maximum(y_at - 1 - source, 0).astype(F32)
        ahead.append(seen * jnp.exp(decay * (-span * gap)))
    total = own_state[...] * whole[0]
    before = jnp.zeros_like(decay)
    for step in range(1, Y_COUNT):
        y_copy(step).wait_recv()
        total = total + row_states[step] * whole[step]
        before = before + row_states[step] * ahead[step]
    row_total[...] = total
    prefix[...] = before

    def z_copy(step):
        return pltpu.make_async_remote_copy(
            src_ref=row_total,
            dst_ref=column_states.at[step],
            send_sem=z_send.at[step],
            recv_sem=z_recv.at[step],
            device_id={"ctx": ctx + step * Y_COUNT},
            device_id_type=MESH,
        )

    def zero_copy(row, column):
        return pltpu.make_async_remote_copy(
            src_ref=row_total,
            dst_ref=zero_state,
            send_sem=zero_send.at[column, row],
            recv_sem=zero_recv,
            device_id={"ctx": row * Y_COUNT + (0 if column else y_at)},
            device_id_type=MESH,
        )

    def zero_arrive():
        zero_copy(z_at, 0).wait_recv()
        near[...] += power[z_at] * zero_state[...]

    def relay_copy(row):
        return pltpu.make_async_remote_copy(
            src_ref=zero_state,
            dst_ref=zero_state,
            send_sem=zero_send.at[0, row],
            recv_sem=zero_recv,
            device_id={"ctx": row * Y_COUNT + y_at},
            device_id_type=MESH,
        )

    def zero_visit(act):
        for row in NEAR + FAR:

            @pl.when(zero_sender)
            def _(row=row):
                act(row, 0)

            @pl.when(zero_double)
            def _(row=row):
                act(row, 1)

    def zero_start(row, column):
        pl.semaphore_wait(zero_ready.at[column, row], 1)
        zero_copy(row, column).start()

    @pl.when(jnp.logical_and(apart, zero))
    def _():
        zero_visit(zero_start)

    near[...] = jnp.zeros_like(decay)

    def arrive(step, carry):
        z_copy(step).wait_recv()
        near[...] += power[step] * column_states[step]
        return carry

    @pl.when(forwards)
    def _():
        lax.fori_loop(1, recv_count + 1, arrive, 0)
        row_total[...] += power[2] * near[...]

    @pl.when(jnp.logical_and(late_member, z_at < last))
    def _():
        pl.semaphore_wait(go, 1)

    @pl.when(early_sender)
    def _():
        def dispatch(step, carry):
            pl.semaphore_wait(ready.at[step], 1)
            z_copy(step).start()
            return carry

        lax.fori_loop(1, send_count + 1, dispatch, 0)

    @pl.when(jnp.logical_not(early_sender))
    def _():
        def dispatch(at, carry):
            z_copy(send_count - at).start()
            return carry

        lax.fori_loop(0, send_count, dispatch, 0)

    @pl.when(relays)
    def _():
        zero_arrive()
        for row in reversed(range(*RELAYED)):
            relay_copy(row).start()

    @pl.when(jnp.logical_not(zero))
    def _():
        convolve()

    @pl.when(jnp.logical_not(forwards))
    def _():
        lax.fori_loop(1, recv_count + 1, arrive, 0)

    @pl.when(jnp.logical_and(from_zero, jnp.logical_not(relays)))
    def _():
        zero_arrive()

    entering = prefix[...] + near[...] * jnp.exp(decay * (-span * y_f))
    near[...] = entering * jnp.exp(-decay)
    modes = [jnp.broadcast_to(near[r : r + 1, :], (ROWS, lane_count)) for r in range(mode_count)]

    def finish(pair, carry):
        tiles = []
        for half in range(2):
            block = 2 * pair + half
            terms = [table[block, r] * modes[r] for r in range(mode_count)]
            terms.append(base[pl.ds(pl.multiple_of(ROWS * block, ROWS), ROWS), :])
            while len(terms) > 1:
                terms = [sum(terms[at : at + 2][1:], terms[at]) for at in range(0, len(terms), 2)]
            tiles.append(terms[0])
        rows = pl.ds(pl.multiple_of(2 * ROWS * pair, 2 * ROWS), 2 * ROWS)
        mixed = query_buf[rows, :].astype(F32) * jnp.concatenate(tiles, axis=0)
        out_buf[rows, :] = mixed.astype(jnp.bfloat16)
        return carry

    lax.fori_loop(0, block_count // 2, finish, 0, unroll=2)
    store = pltpu.make_async_copy(out_buf, out_hbm, store_sem)
    store.start()
    for step in range(1, Y_COUNT):
        y_copy(step).wait_send()

    def drain(step, carry):
        z_copy(step).wait_send()
        return carry

    lax.fori_loop(1, send_count + 1, drain, 0)

    @pl.when(jnp.logical_and(apart, zero))
    def _():
        zero_visit(lambda row, column: zero_copy(row, column).wait_send())

    @pl.when(relays)
    def _():
        for row in range(*RELAYED):
            relay_copy(row).wait_send()

    store.wait()


def local(query_proj, key_proj, value_proj, decays, residues, skip_gain):
    row_count, lane_count = query_proj.shape
    mode_count = decays.shape[1]
    ctx_count = lax.axis_size("ctx")
    z_count = ctx_count // Y_COUNT
    state = (mode_count, lane_count)
    wide = (row_count, lane_count)
    block_count = row_count // ROWS
    any_space = pl.BlockSpec(memory_space=pl.ANY)
    return pl.pallas_call(
        kernel,
        out_shape=jax.ShapeDtypeStruct(wide, jnp.bfloat16),
        in_specs=[any_space] * 6,
        out_specs=any_space,
        scratch_shapes=[
            pltpu.VMEM(wide, jnp.bfloat16),
            pltpu.VMEM(wide, jnp.bfloat16),
            pltpu.VMEM(wide, jnp.bfloat16),
            pltpu.VMEM(state, F32),
            pltpu.VMEM(state, F32),
            pltpu.VMEM((1, lane_count), F32),
            pltpu.VMEM(wide, jnp.bfloat16),
            pltpu.VMEM((64 + row_count, lane_count), F32),
            pltpu.VMEM((ROWS, 56 + row_count, lane_count), F32),
            pltpu.VMEM((block_count, mode_count, ROWS, lane_count), F32),
            pltpu.VMEM(wide, F32),
            pltpu.VMEM(wide, F32),
            pltpu.VMEM(state, F32),
            pltpu.VMEM((z_count,) + state, F32),
            pltpu.VMEM(state, F32),
            pltpu.VMEM(state, F32),
            pltpu.VMEM((Y_COUNT,) + state, F32),
            pltpu.VMEM(state, F32),
            pltpu.VMEM((z_count,) + state, F32),
            pltpu.VMEM(state, F32),
            pltpu.SemaphoreType.DMA((6,)),
            pltpu.SemaphoreType.DMA,
            pltpu.SemaphoreType.DMA((Y_COUNT,)),
            pltpu.SemaphoreType.DMA((Y_COUNT,)),
            pltpu.SemaphoreType.DMA((z_count,)),
            pltpu.SemaphoreType.DMA((z_count,)),
            pltpu.SemaphoreType.REGULAR((Y_COUNT,)),
            pltpu.SemaphoreType.REGULAR((EARLY_END,)),
            pltpu.SemaphoreType.REGULAR,
            pltpu.SemaphoreType.DMA((2, z_count)),
            pltpu.SemaphoreType.DMA,
            pltpu.SemaphoreType.REGULAR((2, z_count)),
        ],
        compiler_params=pltpu.CompilerParams(collective_id=0, has_side_effects=True),
    )(query_proj, key_proj, value_proj, decays.T, residues.T, skip_gain.reshape(1, lane_count))


def solution(mesh):
    return jax.shard_map(
        local,
        mesh=mesh,
        in_specs=(P("ctx", "ch"), P("ctx", "ch"), P("ctx", "ch"), P(), P(), P("ch")),
        out_specs=P("ctx", "ch"),
        check_vma=False,
    )
```

time: 26.3 us -> 18.7 us (0.71)
  the two profiles are of different devices: /device:TPU:4 before, /device:TPU:472 now
where the time goes in v2:
time: 18.7 us; the launch traced here: 18.5 us
  Pallas kernels  17 us (91%)
  local copies, waits for them, and re-layouts  1.47 us (8%)
    pallas_call x1, Pallas kernels, local(): pl.pallas_call(kernel, out_shape=jax.ShapeDtypeStruct(wide, jnp.bfloat16)...  17 us
    unnamed x1, local copies, waits for them, and re-layouts  1.47 us

profile of v2, /device:TPU:472, one launch (start us, length us, event | category | flops | bytes accessed | tf_op | source)
XLA Modules:
  0.0 18.5 jit_solution(98705840014836953)
XLA Ops:
  0.0 17.0 %shard_map.64 = bf16[256,128]{1,0:T(8,128)(2,1)} custom-call(bf16[256,128]{1,0:T(8,128)(2,1)} %query_hbm.1, bf16[256,128]{1,0:T(8,128)(2,1)} %key_hbm.1, bf16[256,128]{1,0:T(8,128)(2,1)} %value_hbm.1, f32[16,1024]{1,0:T(8,128)} %bitcast.3, f32[16,1024]{1,0:T(8,128)} %bitcast.4, f32[1,128]{1,0:T(1,128)} %bitcast.5), custom_call_target="tpu_custom_call" | custom-call | tf_op jit(solution)/shard_map/pallas_call | solution.py:411
  17.0 1.5 %copy.8 = bf16[256,128]{1,0:T(8,128)(2,1)} copy(bf16[256,128]{1,0:T(8,128)(2,1)} %shard_map.64) | data formatting | bytes 131072
